TPU v7x, 512 devices: a whole 4x8x8 slice. The times are simulated.
512 devices in a mesh: blk: 32 (over x_hi, z, core), adp: 16 (over y, x_lo).
Axes of the slice: x: 4 (x_hi: 2, x_lo: 2; x = x_hi * 2 + x_lo), y: 8, z: 8, core: 2. Of those that a mesh axis runs over, the one named last changes fastest.
Arguments:
- stream: bfloat16 [16384, 1536], P(('blk', 'adp')), may hold values from -6 to 6
- prenorm_gain: float32 [1536], replicated, may hold values from 0.25 to 1.75
- gate_up_weight: bfloat16 [2, 4608, 1536], P(None, 'blk'), may hold values from -0.15625 to 0.15625
- down_weight: bfloat16 [4608, 1536], P('blk'), may hold values from -0.09375 to 0.09375
- adapter_gate_input: bfloat16 [64, 32, 1536], P('adp'), may hold values from -0.15625 to 0.15625
- adapter_gate_output: bfloat16 [64, 2, 16, 4608], P('adp', None, None, 'blk'), may hold values from -0.75 to 0.75
- adapter_down_input: bfloat16 [64, 4608, 16], P('adp', 'blk'), may hold values from -0.09375 to 0.09375
- adapter_down_output: bfloat16 [64, 16, 1536], P('adp'), may hold values from -0.75 to 0.75
- adapter_of_request: int32 [256], replicated, may hold values from 0 to 63, as said below
- request_of_slot: int32 [16384], P(('blk', 'adp')), may hold values from 0 to 255
Outputs:
- mixed: bfloat16 [16384, 1536], P(('blk', 'adp'))
Inputs may be any that keep to these rules, and one draw needn't show every extreme that they name: `adapter_of_request`: exactly 16 distinct adapter numbers occur.
All inputs are finite; a program needn't handle non-finite values.
Results may differ from a plain program's by a relative error of at most 0.014.
Values may be sent and summed in bfloat16 or wider, within the bound.
A program may use at most 64 MiB of HBM per device.

v0:
```python
import jax
import jax.numpy as jnp
from jax import lax
from jax.sharding import PartitionSpec as P

ACTIVE = 16
norm_eps = 1e-06


def normalize(rows, gain):
    value_rows = rows.astype(jnp.float32)
    scale = lax.rsqrt(jnp.mean(value_rows * value_rows, axis=-1, keepdims=True) + norm_eps)
    return (value_rows * scale * gain).astype(jnp.bfloat16)


def local(
    stream,
    prenorm_gain,
    gate_up_weight,
    down_weight,
    adapter_gate_input,
    adapter_gate_output,
    adapter_down_input,
    adapter_down_output,
    adapter_of_request,
    request_of_slot,
):
    width = stream.shape[1]
    tok_rows = stream.shape[0]
    hidden_dev = down_weight.shape[0]
    rank_columns = adapter_down_output.shape[1]
    holders = lax.axis_size("adp")
    kept_rows = adapter_gate_input.shape[0]
    catalog = jnp.arange(kept_rows * holders, dtype=jnp.int32)
    used = jnp.any(adapter_of_request[:, None] == catalog[None, :], axis=0)
    order = jnp.cumsum(used.astype(jnp.int32)) - 1
    active_pos = jnp.arange(ACTIVE, dtype=jnp.int32)
    picked = used[None, :] & (order[None, :] == active_pos[:, None])
    active = jnp.sum(jnp.where(picked, catalog[None, :], 0), axis=1)
    every = (
        lax.all_gather(adapter_gate_input, "adp", axis=0, tiled=True),
        lax.all_gather(adapter_gate_output, "adp", axis=0, tiled=True),
        lax.all_gather(adapter_down_input, "adp", axis=0, tiled=True),
        lax.all_gather(adapter_down_output, "adp", axis=0, tiled=True),
    )
    input_factor = jnp.take(every[0], active, axis=0)
    output_factor = jnp.take(every[1], active, axis=0)
    down_input_factor = jnp.take(every[2], active, axis=0)
    down_output_factor = jnp.take(every[3], active, axis=0)
    table = jnp.arange(adapter_of_request.shape[0], dtype=jnp.int32)
    own_adapter = jnp.sum(
        jnp.where(request_of_slot[:, None] == table[None, :], adapter_of_request[None, :], 0),
        axis=1,
    )
    own_match = own_adapter[:, None] == active[None, :]
    own_slot = jnp.sum(jnp.where(own_match, active_pos[None, :], 0), axis=1)
    normed = normalize(stream, prenorm_gain)
    packed = jnp.concatenate(
        [normed, jnp.broadcast_to(own_slot.astype(jnp.bfloat16)[:, None], (tok_rows, 128))], axis=1
    )
    gathered = lax.all_gather(packed, "blk", axis=0, tiled=True)
    all_rows = gathered[:, :width]
    group_match = gathered[:, width : width + 1].astype(jnp.float32) == active_pos.astype(
        jnp.float32
    )
    match_ranks = jnp.repeat(group_match, rank_columns, axis=1)
    cat_rows = ACTIVE * rank_columns
    pre = []
    for side in range(2):
        rows_in = input_factor[:, side * rank_columns : (side + 1) * rank_columns]
        low = lax.dot_general(
            all_rows,
            rows_in.reshape(cat_rows, width),
            (((1,), (1,)), ((), ())),
            preferred_element_type=jnp.float32,
        )
        low_spread = jnp.where(match_ranks, low, 0).astype(jnp.bfloat16)
        base = lax.dot_general(
            all_rows,
            gate_up_weight[side],
            (((1,), (1,)), ((), ())),
            preferred_element_type=jnp.float32,
        )
        pre.append(
            base
            + jnp.dot(
                low_spread,
                output_factor[:, side].reshape(cat_rows, hidden_dev),
                preferred_element_type=jnp.float32,
            )
        )
    hidden = (jax.nn.gelu(pre[0], approximate=True) * pre[1]).astype(jnp.bfloat16)
    down_in = down_input_factor.transpose(1, 0, 2).reshape(hidden_dev, cat_rows)
    partial_value = jnp.dot(hidden, down_in, preferred_element_type=jnp.float32)
    low_spread = jnp.where(match_ranks, partial_value, 0).astype(jnp.bfloat16)
    part = jnp.dot(hidden, down_weight, preferred_element_type=jnp.float32) + jnp.dot(
        low_spread, down_output_factor.reshape(cat_rows, width), preferred_element_type=jnp.float32
    )
    total = lax.psum_scatter(
        part.astype(jnp.bfloat16), "blk", scatter_dimension=0, tiled=True
    ).astype(jnp.float32)
    return (stream.astype(jnp.float32) + total).astype(jnp.bfloat16)


def solution(mesh):
    in_specs = (
        P(("blk", "adp"), None),
        P(),
        P(None, "blk", None),
        P("blk", None),
        P("adp", None, None),
        P("adp", None, None, "blk"),
        P("adp", "blk", None),
        P("adp", None, None),
        P(),
        P(("blk", "adp")),
    )
    out_specs = P(("blk", "adp"), None)
    return jax.shard_map(local, mesh=mesh, in_specs=in_specs, out_specs=out_specs, check_vma=False)
```

profile of v0, /device:TPU:8, one launch (start us, length us, event | category | flops | bytes accessed | tf_op | source)
XLA Modules:
  0.0 529.4 jit_solution(233450659145894325)
XLA Ops:
  6.5 0.0 copy-start
  6.5 0.0 all-gather.8.cloned.1.call-start
  6.5 0.7 all-gather.8.cloned.1.call-update
  7.3 0.0 all-gather.4.cloned.1.call-start
  7.3 0.8 fusion.60
  8.1 0.1 copy.17
  8.2 0.1 reduce-window.8
  8.3 0.1 add_reduce_fusion
  8.4 0.1 select_reduce_fusion.2
  8.5 0.9 select_reduce_fusion
  9.4 0.1 select_reduce_fusion.1
  9.5 1.0 fusion.56
  10.5 1.0 fusion.58
  11.5 0.1 broadcast_in_dim.116
  11.6 0.7 pad_maximum_fusion
  12.3 0.0 all-gather.4.cloned.1.call-update
  12.3 0.0 all-gather.6.cloned.1.call-start
  12.3 0.7 all-gather.6.cloned.1.call-update
  13.0 0.0 reduce-scatter.2.cloned.1.call-start
  13.1 0.1 broadcast_in_dim.125
  13.2 0.1 broadcast_in_dim.126
  13.3 57.1 %all_gather.17 = bf16[64,2,16,144]{3,2,1,0:T(8,128)(2,1)S(1)} all-gather(bf16[4,2,16,144]{3,2,1,0:T(8,128)(2,1)} %param.15), channel_id=1, replica_groups=mesh['blk'=32,'adp'=16] {'adp'}, dimensions={0}, use_global_device_ids=true | all-gather | bytes 626688 | tf_op jit(solution)/shard_map/all_gather | solution.py:42
  70.3 0.6 gather_fusion.1
  70.9 46.0 %all_gather.18 = bf16[64,144,16]{1,2,0:T(8,128)(2,1)S(1)} all-gather(bf16[4,144,16]{1,2,0:T(8,128)(2,1)} %param.16), channel_id=1, replica_groups=mesh['blk'=32,'adp'=16] {'adp'}, dimensions={0}, use_global_device_ids=true | all-gather | bytes 313344 | tf_op jit(solution)/shard_map/all_gather | solution.py:43
  116.9 0.6 gather_fusion.2
  117.5 0.1 broadcast_select_fusion.2
  117.6 0.1 broadcast_select_fusion.1
  117.7 1.6 all-gather.8.cloned.1.call-done
  119.3 2.5 gather_fusion.3
  121.8 0.2 bitcast_select_fusion
  122.0 95.4 %all-gather.4.cloned.1.call-done = bf16[1024,1664]{1,0:T(8,128)(2,1)} async-done(((bf16[32,1664]{1,0:T(8,128)(2,1)}), bf16[1024,1664]{1,0:T(8,128)(2,1)}) %all-gather.4.cloned.1.call-update) | async-done | bytes 3407888 | tf_op jit(solution)/shard_map/all_gather | solution.py:61
  217.3 1.1 convert_reduce_fusion
  218.4 0.1 broadcast_compare_fusion
  218.5 0.1 broadcast_in_dim.117
  218.6 0.3 copy.18
  219.0 140.2 %all-gather.6.cloned.1.call-done = bf16[64,32,1536]{2,1,0:T(8,128)(2,1)} async-done(((bf16[4,32,1536]{2,1,0:T(8,128)(2,1)}), bf16[64,32,1536]{2,1,0:T(8,128)(2,1)}) %all-gather.6.cloned.1.call-update) | async-done | bytes 6291472 | tf_op jit(solution)/shard_map/all_gather | solution.py:41
  359.1 3.4 gather_fusion
  362.6 0.2 broadcast_select_fusion
  362.8 0.1 fusion.66
  362.9 4.0 fusion.34
  366.9 4.2 fusion.46
  371.1 0.0 copy-start.2
  371.1 4.1 fusion.31
  375.1 0.0 copy-done.2
  375.1 3.3 fusion.37
  378.5 4.1 fusion.36
  382.6 0.0 copy-done
  382.6 5.5 %add_convert_fusion = bf16[1024,1536]{1,0:T(8,128)(2,1)} fusion(f32[1024,1536]{1,0:T(8,128)} %fusion.36, bf16[1024,144]{0,1:T(8,128)(2,1)S(1)} %fusion.37, bf16[144,1536]{1,0:T(8,128)(2,1)S(1)} %copy-done), kind=kOutput, calls=%fused_computation.4 | convolution fusion | flops 456130560 | bytes 10174464 | tf_op jit(solution)/shard_map/dot_general | solution.py:96
  388.1 0.0 copy-start.1
  388.1 0.0 reduce-scatter.2.cloned.1.call-update
  388.1 133.2 %reduce-scatter.2.cloned.1.call-done = bf16[32,1536]{1,0:T(8,128)(2,1)} async-done(((bf16[1024,1536]{1,0:T(8,128)(2,1)}), bf16[32,1536]{1,0:T(8,128)(2,1)}) %reduce-scatter.2.cloned.1.call-update) | async-done | bytes 98320 | tf_op jit(solution)/shard_map/reduce_scatter | solution.py:99
  521.3 0.0 copy-done.1
  521.3 1.6 fusion.59
  (8 shorter events, 0.1 us)
Async XLA Ops:
  6.5 376.0 %copy-start = (bf16[144,1536]{1,0:T(8,128)(2,1)S(1)}, bf16[144,1536]{1,0:T(8,128)(2,1)}, u32[]{:S(2)}) copy-start(bf16[144,1536]{1,0:T(8,128)(2,1)} %param.13) | copy-start | bytes 1327108
  6.5 112.8 %all-gather.8.cloned.1.call-start = ((), (), s32[]{:S(2)}) async-start(), calls=%async_computation.3 | async-start | bytes 3342336 | tf_op jit(solution)/shard_map/all_gather | solution.py:44
  7.3 210.1 %all-gather.4.cloned.1.call-start = ((), (), s32[]{:S(2)}) async-start(), calls=%async_computation.1 | async-start | bytes 3514368 | tf_op jit(solution)/shard_map/all_gather | solution.py:61
  12.3 346.8 %all-gather.6.cloned.1.call-start = ((), (), s32[]{:S(2)}) async-start(), calls=%async_computation.2 | async-start | bytes 6684672 | tf_op jit(solution)/shard_map/all_gather | solution.py:41
  13.0 508.3 %reduce-scatter.2.cloned.1.call-start = ((), (), s32[]{:S(2)}) async-start(), calls=%async_computation.4 | async-start | bytes 3244032 | tf_op jit(solution)/shard_map/reduce_scatter | solution.py:99
  371.1 4.1 copy-start.2
  388.1 133.2 %copy-start.1 = (bf16[32,1536]{1,0:T(8,128)(2,1)S(1)}, bf16[32,1536]{1,0:T(8,128)(2,1)}, u32[]{:S(2)}) copy-start(bf16[32,1536]{1,0:T(8,128)(2,1)} %param.10) | copy-start | bytes 294916
Sparse Core Ops, SparseCore 0:
  9.4 109.8 all-gather.7
  122.7 94.6 all-gather.3
  219.4 139.6 all-gather.5
  388.2 133.0 reduce-scatter.1
where the time goes:
time: 530 us; the launch traced here: 529 us
  waiting for transfers between devices  372 us (70%)
  blocking collectives  103 us (19%)
  matrix products  25.2 us (5%)
  between operations  13.3 us (3%)
  other arithmetic  8.07 us (2%)
  local copies, waits for them, and re-layouts  7.92 us (1%)
    all_gather x1, waiting for transfers between devices, local(): lax.all_gather(adapter_gate_input, 'adp', axis=0, tiled=True)  140 us
    reduce_scatter x1, waiting for transfers between devices, local(): lax.psum_scatter(part.astype(jnp.bfloat16), 'blk', scatter_dimension=0, t...  133 us
    all_gather x1, waiting for transfers between devices, local(): gathered = lax.all_gather(packed, 'blk', axis=0, tiled=True)  95.4 us
    all_gather x1, blocking collectives, local(): lax.all_gather(adapter_gate_output, 'adp', axis=0, tiled=True)  57.1 us
    all_gather x1, blocking collectives, local(): lax.all_gather(adapter_down_input, 'adp', axis=0, tiled=True)  46 us
  transfers between devices with their start and end apart: 4, of which 4 were waited for; matrix products, arithmetic and copies ran while one was open for 2% of the time, Pallas kernels for 0%

commit v1 on v0

--- a/solution.py
+++ b/solution.py
@@ -37,8 +37,14 @@
     active_pos = jnp.arange(ACTIVE, dtype=jnp.int32)
     picked = used[None, :] & (order[None, :] == active_pos[:, None])
     active = jnp.sum(jnp.where(picked, catalog[None, :], 0), axis=1)
+
+    def convert_leaf(x_in):
+        return jnp.concatenate(
+            lax.all_to_all(jnp.stack(lax.axis_size("adp") * [x_in]), "adp", 0, 0), 0
+        )
+
     every = (
-        lax.all_gather(adapter_gate_input, "adp", axis=0, tiled=True),
+        convert_leaf(adapter_gate_input),
         lax.all_gather(adapter_gate_output, "adp", axis=0, tiled=True),
         lax.all_gather(adapter_down_input, "adp", axis=0, tiled=True),
         lax.all_gather(adapter_down_output, "adp", axis=0, tiled=True),

time: 530 us -> 482 us (0.909)
  waiting for transfers between devices: 372 us -> 171 us
  blocking collectives: 103 us -> 244 us
  starting transfers between devices: 0.12 us -> 10.4 us
    all_gather x1, blocking collectives: 57.1 us -> 211 us  [local(): lax.all_gather(adapter_gate_output, 'adp', axis=0, tiled=True)]
    all_gather x1 -> x0, waiting for transfers between devices: 140 us -> none  [local(): lax.all_gather(adapter_gate_input, 'adp', axis=0, tiled=True)]
    all_gather x1, waiting for transfers between devices: 95.4 us -> 41.8 us  [local(): gathered = lax.all_gather(packed, 'blk', axis=0, tiled=True)]
    all_gather x1, blocking collectives: 46 us -> 33.1 us  [local(): lax.all_gather(adapter_down_input, 'adp', axis=0, tiled=True)]
    all_to_all x0 -> x1, starting transfers between devices: none -> 10.3 us  [convert_leaf(): lax.all_to_all(jnp.stack(lax.axis_size('adp') * [x_in]), 'adp', 0, 0)]
  transfers between devices with their start and end apart: 4 -> 4, of which waited for: 4 -> 2; matrix products, arithmetic and copies ran while one was open for 2% -> 2% of each run, Pallas kernels for 0% -> 0%
where the time goes in v1:
time: 482 us; the launch traced here: 481 us
  blocking collectives  244 us (51%)
  waiting for transfers between devices  171 us (35%)
  matrix products  24.2 us (5%)
  between operations  13.4 us (3%)
  local copies, waits for them, and re-layouts  12.5 us (3%)
  starting transfers between devices  10.4 us (2%)
  other arithmetic  5.53 us (1%)
    all_gather x1, blocking collectives, local(): lax.all_gather(adapter_gate_output, 'adp', axis=0, tiled=True)  211 us
    reduce_scatter x1, waiting for transfers between devices, local(): lax.psum_scatter(part.astype(jnp.bfloat16), 'blk', scatter_dimension=0, t...  129 us
    all_gather x1, waiting for transfers between devices, local(): gathered = lax.all_gather(packed, 'blk', axis=0, tiled=True)  41.8 us
    all_gather x1, blocking collectives, local(): lax.all_gather(adapter_down_input, 'adp', axis=0, tiled=True)  33.1 us
    all_to_all x1, starting transfers between devices, convert_leaf(): lax.all_to_all(jnp.stack(lax.axis_size('adp') * [x_in]), 'adp', 0, 0)  10.3 us
  transfers between devices with their start and end apart: 4, of which 2 were waited for; matrix products, arithmetic and copies ran while one was open for 2% of the time, Pallas kernels for 0%

profile of v1, /device:TPU:8, one launch (start us, length us, event | category | flops | bytes accessed | tf_op | source)
XLA Modules:
  0.0 481.4 jit_solution(11043996429032792005)
XLA Ops:
  6.5 0.0 copy-start
  6.5 0.0 all-gather.5.cloned.1.call-start
  6.5 0.7 all-gather.5.cloned.1.call-update
  7.3 4.4 stack.2
  11.7 0.0 copy-start.7
  11.7 0.0 copy-start.8
  11.7 0.0 copy-start.1
  11.7 0.0 copy-start.2
  11.7 0.0 copy-start.3
  11.7 10.3 %all-to-all-start = ((bf16[16,4,32,1536]{3,2,1,0:T(8,128)(2,1)}), bf16[16,4,32,1536]{3,2,1,0:T(8,128)(2,1)}, u32[]{:S(2)}, u32[]{:S(2)}) async-start(bf16[16,4,32,1536]{3,2,1,0:T(8,128)(2,1)} %stack.2), calls=%async_computation | async-start | bytes 12582912 | tf_op jit(solution)/shard_map/all_to_all | solution.py:43
  22.0 0.0 all-gather.3.cloned.1.call-start
  22.1 0.0 copy-done.7
  22.1 0.1 fusion.60
  22.2 0.1 copy.17
  22.3 0.1 reduce-window.8
  22.4 0.1 add_reduce_fusion
  22.5 0.1 select_reduce_fusion.2
  22.6 0.0 copy-done.8
  22.7 0.2 select_reduce_fusion
  22.8 0.1 select_reduce_fusion.1
  22.9 0.0 copy-done.1
  23.0 0.1 fusion.56
  23.1 0.0 copy-done.5
  23.1 0.1 fusion.58
  23.2 0.1 broadcast_in_dim.116
  23.3 0.6 pad_maximum_fusion
  23.9 0.0 all-gather.3.cloned.1.call-update
  23.9 0.0 reduce-scatter.2.cloned.1.call-start
  24.0 0.0 copy-start.6
  24.0 0.1 broadcast_in_dim.125
  24.1 0.1 broadcast_in_dim.126
  24.2 0.0 copy-done.2
  24.2 0.0 copy-start.4
  24.2 211.0 %all_gather.13 = bf16[64,2,16,144]{3,2,1,0:T(8,128)(2,1)S(1)} all-gather(bf16[4,2,16,144]{3,2,1,0:T(8,128)(2,1)S(1)} %copy-done.2), channel_id=1, replica_groups=mesh['blk'=32,'adp'=16] {'adp'}, dimensions={0}, use_global_device_ids=true | all-gather | bytes 626688 | tf_op jit(solution)/shard_map/all_gather | solution.py:48
  235.2 0.6 gather_fusion.1
  235.8 0.0 copy-done.3
  235.8 33.1 %all_gather.14 = bf16[64,144,16]{1,2,0:T(8,128)(2,1)S(1)} all-gather(bf16[4,144,16]{1,2,0:T(8,128)(2,1)S(1)} %copy-done.3), channel_id=1, replica_groups=mesh['blk'=32,'adp'=16] {'adp'}, dimensions={0}, use_global_device_ids=true | all-gather | bytes 313344 | tf_op jit(solution)/shard_map/all_gather | solution.py:49
  268.9 0.6 gather_fusion.2
  269.4 0.1 broadcast_select_fusion.2
  269.5 0.1 broadcast_select_fusion.1
  269.6 0.0 copy-done.6
  269.7 0.0 all-gather.5.cloned.1.call-done
  269.7 2.5 gather_fusion.3
  272.2 0.2 bitcast_select_fusion
  272.3 0.0 copy-done.4
  272.4 41.8 %all-gather.3.cloned.1.call-done = bf16[1024,1664]{1,0:T(8,128)(2,1)} async-done(((bf16[32,1664]{1,0:T(8,128)(2,1)}), bf16[1024,1664]{1,0:T(8,128)(2,1)}) %all-gather.3.cloned.1.call-update) | async-done | bytes 3407888 | tf_op jit(solution)/shard_map/all_gather | solution.py:67
  314.2 1.1 convert_reduce_fusion
  315.3 0.1 broadcast_compare_fusion
  315.3 0.1 broadcast_in_dim.117
  315.4 0.3 copy.18
  315.8 0.0 all-to-all-done
  315.8 3.6 gather_fusion
  319.4 0.8 broadcast_select_fusion
  320.2 0.1 fusion.66
  320.3 4.0 fusion.34
  324.3 3.4 fusion.46
  327.7 4.0 fusion.31
  331.7 3.3 fusion.37
  335.0 4.1 fusion.36
  339.1 0.0 copy-done
  339.1 5.5 %add_convert_fusion = bf16[1024,1536]{1,0:T(8,128)(2,1)} fusion(f32[1024,1536]{1,0:T(8,128)} %fusion.36, bf16[1024,144]{0,1:T(8,128)(2,1)S(1)} %fusion.37, bf16[144,1536]{1,0:T(8,128)(2,1)S(1)} %copy-done), kind=kOutput, calls=%fused_computation.4 | convolution fusion | flops 456130560 | bytes 10174464 | tf_op jit(solution)/shard_map/dot_general | solution.py:102
  344.6 0.0 reduce-scatter.2.cloned.1.call-update
  344.6 128.6 %reduce-scatter.2.cloned.1.call-done = bf16[32,1536]{1,0:T(8,128)(2,1)} async-done(((bf16[1024,1536]{1,0:T(8,128)(2,1)}), bf16[32,1536]{1,0:T(8,128)(2,1)}) %reduce-scatter.2.cloned.1.call-update) | async-done | bytes 98320 | tf_op jit(solution)/shard_map/reduce_scatter | solution.py:105
  473.3 1.6 fusion.59
  (9 shorter events, 0.1 us)
Async XLA Ops:
  6.5 332.5 %copy-start = (bf16[144,1536]{1,0:T(8,128)(2,1)S(1)}, bf16[144,1536]{1,0:T(8,128)(2,1)}, u32[]{:S(2)}) copy-start(bf16[144,1536]{1,0:T(8,128)(2,1)} %param.13) | copy-start | bytes 1327108
  6.5 263.1 %all-gather.5.cloned.1.call-start = ((), (), s32[]{:S(2)}) async-start(), calls=%async_computation.3 | async-start | bytes 3342336 | tf_op jit(solution)/shard_map/all_gather | solution.py:50
  11.7 10.4 %copy-start.7 = (s32[256]{0:T(256)S(1)}, s32[256]{0:T(256)}, u32[]{:S(2)}) copy-start(s32[256]{0:T(256)} %param.18) | copy-start | bytes 3076
  11.7 11.0 %copy-start.8 = (s32[32]{0:T(128)S(1)}, s32[32]{0:T(128)}, u32[]{:S(2)}) copy-start(s32[32]{0:T(128)} %param.19) | copy-start | bytes 388
  11.7 11.3 %copy-start.1 = (bf16[32,1536]{1,0:T(8,128)(2,1)S(1)}, bf16[32,1536]{1,0:T(8,128)(2,1)}, u32[]{:S(2)}) copy-start(bf16[32,1536]{1,0:T(8,128)(2,1)} %param.10) | copy-start | bytes 294916
  11.7 11.4 %copy-start.5 = (f32[1536]{0:T(1024)S(1)}, f32[1536]{0:T(1024)}, u32[]{:S(2)}) copy-start(f32[1536]{0:T(1024)} %param.11) | copy-start | bytes 18436
  11.7 12.5 %copy-start.2 = (bf16[4,2,16,144]{3,2,1,0:T(8,128)(2,1)S(1)}, bf16[4,2,16,144]{3,2,1,0:T(8,128)(2,1)}, u32[]{:S(2)}) copy-start(bf16[4,2,16,144]{3,2,1,0:T(8,128)(2,1)} %param.15) | copy-start | bytes 110596
  11.7 224.1 %copy-start.3 = (bf16[4,144,16]{1,2,0:T(8,128)(2,1)S(1)}, bf16[4,144,16]{1,2,0:T(8,128)(2,1)}, u32[]{:S(2)}) copy-start(bf16[4,144,16]{1,2,0:T(8,128)(2,1)} %param.16) | copy-start | bytes 55300
  11.7 304.1 %all-to-all-start = ((bf16[16,4,32,1536]{3,2,1,0:T(8,128)(2,1)}), bf16[16,4,32,1536]{3,2,1,0:T(8,128)(2,1)}, u32[]{:S(2)}, u32[]{:S(2)}) async-start(bf16[16,4,32,1536]{3,2,1,0:T(8,128)(2,1)} %stack.2), calls=%async_computation | async-start | bytes 12582912 | tf_op jit(solution)/shard_map/all_to_all | solution.py:43
  22.0 292.1 %all-gather.3.cloned.1.call-start = ((), (), s32[]{:S(2)}) async-start(), calls=%async_computation.2 | async-start | bytes 3514368 | tf_op jit(solution)/shard_map/all_gather | solution.py:67
  23.9 449.3 %reduce-scatter.2.cloned.1.call-start = ((), (), s32[]{:S(2)}) async-start(), calls=%async_computation.4 | async-start | bytes 3244032 | tf_op jit(solution)/shard_map/reduce_scatter | solution.py:105
  24.0 245.6 %copy-start.6 = (pred[16]{0:T(512)(128)(4,1)}, pred[16]{0:T(512)(128)(4,1)S(1)}, u32[]{:S(2)}) copy-start(pred[16]{0:T(512)(128)(4,1)S(1)} %compare_and_fusion) | copy-start | bytes 52
  24.2 248.1 %copy-start.4 = (s32[1024]{0:T(1024)}, s32[1024]{0:T(1024)S(1)}, u32[]{:S(2)}) copy-start(s32[1024]{0:T(1024)S(1)} %pad_clamp_fusion) | copy-start | bytes 12292
Sparse Core Ops, SparseCore 0:
  9.4 194.9 all-gather.4
  207.8 106.3 all-gather.2
  344.7 128.4 reduce-scatter.1
